TPU v7x, 32 devices: a whole 2x2x4 slice. The times are simulated.
32 devices in a mesh: rows: 4 (over y, x), mp: 8 (over z, core).
Axes of the slice: x: 2, y: 2, z: 4, core: 2. Of those that a mesh axis runs over, the one named last changes fastest.
Arguments:
- inputs: bfloat16 [8192, 2048], P(('rows', 'mp')), may hold values from -6 to 6
- cotangent: bfloat16 [8192, 2048], P(('rows', 'mp')), may hold values from -6 to 6
- corpus_ids: int32 [4], P('rows'), may hold values from 0 to 3
- corpus_weight: float32 [4], replicated, may hold values from 0.5 to 2
- attn_gain: bfloat16 [2048], P(('rows', 'mp')), may hold values from 0.099609375 to 1.8984375
- qkv_weight: bfloat16 [2048, 1920], P(('rows', 'mp')), may hold values from -0.125 to 0.125
- out_weight: bfloat16 [1280, 2048], P(('rows', 'mp')), may hold values from -2.5 to 2.5
- ffn_gain: bfloat16 [2048], P(('rows', 'mp')), may hold values from 0.099609375 to 1.8984375
- gate_weight: bfloat16 [2048, 6144], P(None, 'mp'), may hold values from -0.125 to 0.125
- up_weight: bfloat16 [2048, 6144], P(None, 'mp'), may hold values from -0.125 to 0.125
- down_weight: bfloat16 [6144, 2048], P('mp'), may hold values from -0.078125 to 0.078125
Outputs:
- outputs: bfloat16 [8192, 2048], P(('rows', 'mp'))
- input_grad: float32 [8192, 2048], P(('rows', 'mp'))
- qkv_grad: float32 [2048, 1920], P(('rows', 'mp'))
- proj_grad: float32 [1280, 2048], P(('rows', 'mp'))
- gate_grad: float32 [2048, 6144], P(None, 'mp')
- up_grad: float32 [2048, 6144], P(None, 'mp')
- down_grad: float32 [6144, 2048], P('mp')
- attn_gain_grad: float32 [2048], P(('rows', 'mp'))
- ffn_gain_grad: float32 [2048], P(('rows', 'mp'))
All inputs are finite; a program needn't handle non-finite values.
Results may differ from a plain program's by a relative error of at most 0.015.
Values may be sent and summed in bfloat16 or wider, within the bound.
A program may use at most 256 MiB of HBM per device.

v0:
```python
import jax
import jax.numpy as jnp
from jax import lax
from jax.sharding import PartitionSpec as P

HEADS = 20
KV_HEADS = 5
HEAD_DIM = 64
LEN = 2048
QBLOCK = 512
QBLOCKS = 4
EPS = 1e-05
THETA = 10000.0


def rotation(positions):
    half_dim = HEAD_DIM // 2
    freqs = jnp.exp(-jnp.log(THETA) * (2.0 * jnp.arange(half_dim, dtype=jnp.float32)) / HEAD_DIM)
    angles = positions.astype(jnp.float32)[:, None] * freqs[None, :]
    return (jnp.cos(angles), jnp.sin(angles))


def rotate(values_in, cosine, sine_part):
    half_dim = HEAD_DIM // 2
    first = values_in[..., :half_dim]
    second = values_in[..., half_dim:]
    return jnp.concatenate(
        [first * cosine - second * sine_part, second * cosine + first * sine_part], axis=-1
    )


def rotate_back(values_in, cosine, sine_part):
    half_dim = HEAD_DIM // 2
    first = values_in[..., :half_dim]
    second = values_in[..., half_dim:]
    return jnp.concatenate(
        [first * cosine + second * sine_part, second * cosine - first * sine_part], axis=-1
    )


def project_kv(normed, weight_kv, positions):
    row_count = normed.shape[0]
    kv_width = KV_HEADS * HEAD_DIM
    kv_raw = jnp.dot(normed, weight_kv, preferred_element_type=jnp.float32)
    cosine, sine_part = rotation(positions)
    keys_part = rotate(
        kv_raw[:, :kv_width].reshape(row_count, KV_HEADS, HEAD_DIM),
        cosine[:, None, :],
        sine_part[:, None, :],
    )
    return jnp.concatenate(
        [keys_part.reshape(row_count, kv_width), kv_raw[:, kv_width:]], axis=1
    ).astype(jnp.bfloat16)


def key_slices(kv_all, seq_start, kv_head, length):
    keys_part = lax.dynamic_slice(kv_all, (seq_start, kv_head * HEAD_DIM), (length, HEAD_DIM))
    values_part = lax.dynamic_slice(
        kv_all, (seq_start, (KV_HEADS + kv_head) * HEAD_DIM), (length, HEAD_DIM)
    )
    return (keys_part, values_part)


def masked_scores(queries, keys_part, block_index, length):
    scores = jnp.einsum(
        "qd,kd->qk", queries, keys_part, preferred_element_type=jnp.float32
    ) * HEAD_DIM ** (-0.5)
    allowed = jnp.arange(length)[None, :] <= block_index * QBLOCK + jnp.arange(QBLOCK)[:, None]
    return jnp.where(allowed, scores, -1e30)


def forward_branch(block_index):
    length = (block_index + 1) * QBLOCK

    def branch(queries, kv_all, seq_start, kv_head):
        keys_part, values_part = key_slices(kv_all, seq_start, kv_head, length)
        scores = masked_scores(queries, keys_part, block_index, length)
        row_max = jnp.max(scores, axis=1, keepdims=True)
        exponent = jnp.exp(scores - row_max)
        row_total = jnp.sum(exponent, axis=1, keepdims=True)
        probabilities = (exponent / row_total).astype(jnp.bfloat16)
        output = jnp.dot(probabilities, values_part, preferred_element_type=jnp.float32).astype(
            jnp.bfloat16
        )
        return (output, (row_max + jnp.log(row_total))[:, 0])

    return branch


def backward_branch(block_index):
    length = (block_index + 1) * QBLOCK

    def branch(queries, grad_output, log_total, kv_all, seq_start, kv_head):
        keys_part, values_part = key_slices(kv_all, seq_start, kv_head, length)
        scores = masked_scores(queries, keys_part, block_index, length)
        probabilities = jnp.exp(scores - log_total[:, None])
        grad_probs = jnp.einsum(
            "qd,kd->qk", grad_output, values_part, preferred_element_type=jnp.float32
        )
        row_delta = jnp.sum(probabilities * grad_probs, axis=1, keepdims=True)
        grad_scores = (probabilities * (grad_probs - row_delta)).astype(jnp.bfloat16)
        grad_queries = jnp.dot(
            grad_scores, keys_part, preferred_element_type=jnp.float32
        ) * HEAD_DIM ** (-0.5)
        grad_keys = jnp.einsum(
            "qk,qd->kd", grad_scores, queries, preferred_element_type=jnp.float32
        ) * HEAD_DIM ** (-0.5)
        grad_values = jnp.einsum(
            "qk,qd->kd",
            probabilities.astype(jnp.bfloat16),
            grad_output,
            preferred_element_type=jnp.float32,
        )
        padding = ((0, LEN - length), (0, 0))
        return (grad_queries, jnp.pad(grad_keys, padding), jnp.pad(grad_values, padding))

    return branch


def add_window(target, update, start_row, start_col):
    current = lax.dynamic_slice(target, (start_row, start_col), update.shape)
    return lax.dynamic_update_slice(target, current + update, (start_row, start_col))


def on_device(
    inputs,
    cotangent,
    corpus_ids,
    corpus_weight,
    attn_gain,
    qkv_weight,
    out_weight,
    ffn_gain,
    gate_weight,
    up_weight,
    down_weight,
):
    tok_dev = inputs.shape[0]
    group_rows = tok_dev * lax.axis_size("mp")
    offset = lax.axis_index("mp") * tok_dev
    seq_group = corpus_ids.shape[0]
    corpora_count = corpus_weight.shape[0]
    sequences_all = seq_group * lax.axis_size("rows")
    q_width = HEADS * HEAD_DIM
    kv_width = KV_HEADS * HEAD_DIM
    group_size = HEADS // KV_HEADS
    model_width = inputs.shape[1]
    tiles_dev = HEADS * QBLOCKS // lax.axis_size("mp")
    first_tile = lax.axis_index("mp") * tiles_dev
    chosen = (corpus_ids[:, None] == jnp.arange(corpora_count)[None, :]).astype(jnp.float32)
    counts = lax.psum(jnp.sum(chosen, axis=0), "rows")
    count_seq = jnp.sum(chosen * counts[None, :], axis=1)
    weight_seq = jnp.sum(chosen * corpus_weight[None, :], axis=1)
    seq_scale = weight_seq * sequences_all / (corpora_count * count_seq)
    qkv_full, out_full, gain_one, gain_two = (
        lax.all_gather(qkv_weight, ("rows", "mp"), axis=0, tiled=True),
        lax.all_gather(out_weight, ("rows", "mp"), axis=0, tiled=True),
        lax.all_gather(attn_gain, ("rows", "mp"), axis=0, tiled=True),
        lax.all_gather(ffn_gain, ("rows", "mp"), axis=0, tiled=True),
    )
    gain_one = gain_one.astype(jnp.float32)
    gain_two = gain_two.astype(jnp.float32)
    weight_kv = qkv_full[:, q_width:]
    residual = inputs.astype(jnp.float32)
    inverse_one = lax.rsqrt(jnp.mean(residual * residual, axis=-1, keepdims=True) + EPS)
    normed_one = (residual * inverse_one * gain_one).astype(jnp.bfloat16)
    local_pos = (offset + jnp.arange(tok_dev)) % LEN
    normed_all, kv_all = (
        lax.all_gather(normed_one, "mp", axis=0, tiled=True),
        lax.all_gather(project_kv(normed_one, weight_kv, local_pos), "mp", axis=0, tiled=True),
    )
    count_items = tiles_dev * seq_group
    forward_list = [forward_branch(b) for b in range(QBLOCKS)]
    backward_list = [backward_branch(b) for b in range(QBLOCKS)]

    def item_info(item_index):
        tile_index = first_tile + item_index // seq_group
        seq_start = item_index % seq_group * LEN
        head_index = tile_index // QBLOCKS
        block_index = tile_index % QBLOCKS
        return (head_index, block_index, seq_start, seq_start + block_index * QBLOCK)

    def forward_item(partial_value, item_index):
        head_index, block_index, seq_start, row_start = item_info(item_index)
        rows_in = lax.dynamic_slice(normed_all, (row_start, 0), (QBLOCK, model_width))
        weight_q = lax.dynamic_slice(qkv_full, (0, head_index * HEAD_DIM), (model_width, HEAD_DIM))
        raw_queries = jnp.dot(rows_in, weight_q, preferred_element_type=jnp.float32)
        cosine, sine_part = rotation(block_index * QBLOCK + jnp.arange(QBLOCK))
        queries = rotate(raw_queries, cosine, sine_part).astype(jnp.bfloat16)
        output, log_total = lax.switch(
            block_index, forward_list, queries, kv_all, seq_start, head_index // group_size
        )
        weight_o = lax.dynamic_slice(out_full, (head_index * HEAD_DIM, 0), (HEAD_DIM, model_width))
        partial_value = add_window(
            partial_value,
            jnp.dot(output, weight_o, preferred_element_type=jnp.float32),
            row_start,
            0,
        )
        return (partial_value, (queries, output, log_total))

    attn_partial, (kept_queries, kept_outputs, kept_totals) = lax.scan(
        forward_item, jnp.zeros((group_rows, model_width), jnp.float32), jnp.arange(count_items)
    )
    attn_sum = lax.psum_scatter(attn_partial, "mp", scatter_dimension=0, tiled=True)
    middle = residual + attn_sum
    inverse_two = lax.rsqrt(jnp.mean(middle * middle, axis=-1, keepdims=True) + EPS)
    normed_two = (middle * inverse_two * gain_two).astype(jnp.bfloat16)
    normed_mid = lax.all_gather(normed_two, "mp", axis=0, tiled=True)
    gate_val = jnp.dot(normed_mid, gate_weight, preferred_element_type=jnp.float32)
    up_val = jnp.dot(normed_mid, up_weight, preferred_element_type=jnp.float32)
    hidden = (jax.nn.silu(gate_val) * up_val).astype(jnp.bfloat16)
    ffn_part = jnp.dot(hidden, down_weight, preferred_element_type=jnp.float32)
    ffn_sum = lax.psum_scatter(
        ffn_part.astype(jnp.bfloat16), "mp", scatter_dimension=0, tiled=True
    ).astype(jnp.float32)
    outputs = (middle + ffn_sum).astype(jnp.bfloat16)
    seq_local = (offset + jnp.arange(tok_dev)) // LEN
    token_scale = jnp.sum(
        (seq_local[:, None] == jnp.arange(seq_group)[None, :]).astype(jnp.float32)
        * seq_scale[None, :],
        axis=1,
    )
    grad_out = cotangent.astype(jnp.float32) * token_scale[:, None]
    grad_all = lax.all_gather(grad_out.astype(jnp.bfloat16), "mp", axis=0, tiled=True)
    grad_hidden = jnp.einsum("td,fd->tf", grad_all, down_weight, preferred_element_type=jnp.float32)
    down_grad = jnp.einsum("tf,td->fd", hidden, grad_all, preferred_element_type=jnp.float32)
    sigmoid_val = jax.nn.sigmoid(gate_val)
    grad_gate = (
        grad_hidden * up_val * (sigmoid_val * (1.0 + gate_val * (1.0 - sigmoid_val)))
    ).astype(jnp.bfloat16)
    grad_up = (grad_hidden * (gate_val * sigmoid_val)).astype(jnp.bfloat16)
    gate_grad = jnp.einsum("td,tf->df", normed_mid, grad_gate, preferred_element_type=jnp.float32)
    up_grad = jnp.einsum("td,tf->df", normed_mid, grad_up, preferred_element_type=jnp.float32)
    mid_partial = jnp.einsum(
        "tf,df->td", grad_gate, gate_weight, preferred_element_type=jnp.float32
    )
    mid_partial = mid_partial + jnp.einsum(
        "tf,df->td", grad_up, up_weight, preferred_element_type=jnp.float32
    )
    grad_normed_two = lax.psum_scatter(mid_partial, "mp", scatter_dimension=0, tiled=True)
    scaled_two = grad_normed_two * gain_two
    ffn_gain_part = jnp.sum(grad_normed_two * middle * inverse_two, axis=0)
    grad_middle = (
        grad_out
        + inverse_two * scaled_two
        - middle * inverse_two**3 * jnp.mean(scaled_two * middle, axis=-1, keepdims=True)
    )
    grad_attn_all = lax.all_gather(grad_middle.astype(jnp.bfloat16), "mp", axis=0, tiled=True)

    def backward_item(carried, item_index):
        input_partial, kv_partial, q_grad_w, o_grad_w = carried
        head_index, block_index, seq_start, row_start = item_info(item_index)
        queries = kept_queries[item_index]
        output = kept_outputs[item_index]
        log_total = kept_totals[item_index]
        grad_rows = lax.dynamic_slice(grad_attn_all, (row_start, 0), (QBLOCK, model_width))
        weight_o = lax.dynamic_slice(out_full, (head_index * HEAD_DIM, 0), (HEAD_DIM, model_width))
        grad_output = jnp.einsum(
            "td,hd->th", grad_rows, weight_o, preferred_element_type=jnp.float32
        ).astype(jnp.bfloat16)
        o_grad_w = add_window(
            o_grad_w,
            jnp.einsum("th,td->hd", output, grad_rows, preferred_element_type=jnp.float32),
            head_index * HEAD_DIM,
            0,
        )
        kv_head = head_index // group_size
        grad_queries, grad_keys, grad_values = lax.switch(
            block_index, backward_list, queries, grad_output, log_total, kv_all, seq_start, kv_head
        )
        cosine, sine_part = rotation(block_index * QBLOCK + jnp.arange(QBLOCK))
        grad_raw = rotate_back(grad_queries, cosine, sine_part).astype(jnp.bfloat16)
        rows_in = lax.dynamic_slice(normed_all, (row_start, 0), (QBLOCK, model_width))
        weight_q = lax.dynamic_slice(qkv_full, (0, head_index * HEAD_DIM), (model_width, HEAD_DIM))
        input_partial = add_window(
            input_partial,
            jnp.einsum("th,dh->td", grad_raw, weight_q, preferred_element_type=jnp.float32),
            row_start,
            0,
        )
        q_grad_w = add_window(
            q_grad_w,
            jnp.einsum("td,th->dh", rows_in, grad_raw, preferred_element_type=jnp.float32),
            0,
            head_index * HEAD_DIM,
        )
        kv_partial = add_window(kv_partial, grad_keys, seq_start, kv_head * HEAD_DIM)
        kv_partial = add_window(kv_partial, grad_values, seq_start, (KV_HEADS + kv_head) * HEAD_DIM)
        return ((input_partial, kv_partial, q_grad_w, o_grad_w), None)

    start_state = (
        jnp.zeros((group_rows, model_width), jnp.float32),
        jnp.zeros((group_rows, 2 * kv_width), jnp.float32),
        jnp.zeros((model_width, q_width), jnp.float32),
        jnp.zeros((q_width, model_width), jnp.float32),
    )
    (input_partial, kv_partial, q_grad_w, o_grad_w), unused = lax.scan(
        backward_item, start_state, jnp.arange(count_items)
    )
    input_sum, kv_sum = (
        lax.psum_scatter(input_partial, "mp", scatter_dimension=0, tiled=True),
        lax.psum_scatter(kv_partial, "mp", scatter_dimension=0, tiled=True),
    )
    cos_local, sin_local = rotation(local_pos)
    grad_keys_local = rotate_back(
        kv_sum[:, :kv_width].reshape(tok_dev, KV_HEADS, HEAD_DIM),
        cos_local[:, None, :],
        sin_local[:, None, :],
    )
    grad_kv = jnp.concatenate(
        [grad_keys_local.reshape(tok_dev, kv_width), kv_sum[:, kv_width:]], axis=1
    ).astype(jnp.bfloat16)
    grad_normed_one = input_sum + jnp.einsum(
        "tk,dk->td", grad_kv, weight_kv, preferred_element_type=jnp.float32
    )
    kv_grad_w = jnp.einsum("td,tk->dk", normed_one, grad_kv, preferred_element_type=jnp.float32)
    qkv_grad_full = jnp.concatenate([q_grad_w, kv_grad_w], axis=1)
    scaled_one = grad_normed_one * gain_one
    attn_gain_part = jnp.sum(grad_normed_one * residual * inverse_one, axis=0)
    input_grad = (
        grad_middle
        + inverse_one * scaled_one
        - residual * inverse_one**3 * jnp.mean(scaled_one * residual, axis=-1, keepdims=True)
    )
    qkv_grad, proj_grad, attn_gain_grad, ffn_gain_grad = (
        lax.psum_scatter(qkv_grad_full, ("rows", "mp"), scatter_dimension=0, tiled=True),
        lax.psum_scatter(o_grad_w, ("rows", "mp"), scatter_dimension=0, tiled=True),
        lax.psum_scatter(attn_gain_part, ("rows", "mp"), scatter_dimension=0, tiled=True),
        lax.psum_scatter(ffn_gain_part, ("rows", "mp"), scatter_dimension=0, tiled=True),
    )
    gate_grad, up_grad, down_grad = (
        lax.psum(gate_grad.astype(jnp.bfloat16), "rows").astype(jnp.float32),
        lax.psum(up_grad.astype(jnp.bfloat16), "rows").astype(jnp.float32),
        lax.psum(down_grad.astype(jnp.bfloat16), "rows").astype(jnp.float32),
    )
    return (
        outputs,
        input_grad,
        qkv_grad,
        proj_grad,
        gate_grad,
        up_grad,
        down_grad,
        attn_gain_grad,
        ffn_gain_grad,
    )


def solution(mesh):
    in_specs = (
        P(("rows", "mp"), None),
        P(("rows", "mp"), None),
        P("rows"),
        P(),
        P(("rows", "mp")),
        P(("rows", "mp"), None),
        P(("rows", "mp"), None),
        P(("rows", "mp")),
        P(None, "mp"),
        P(None, "mp"),
        P("mp", None),
    )
    out_specs = (
        P(("rows", "mp"), None),
        P(("rows", "mp"), None),
        P(("rows", "mp"), None),
        P(("rows", "mp"), None),
        P(None, "mp"),
        P(None, "mp"),
        P("mp", None),
        P(("rows", "mp")),
        P(("rows", "mp")),
    )
    return jax.shard_map(
        on_device, mesh=mesh, in_specs=in_specs, out_specs=out_specs, check_vma=False
    )
```

profile of v0, /device:TPU:0, one launch (start us, length us, event | category | flops | bytes accessed | tf_op | source)
XLA Modules:
  0.0 2238.0 jit_solution(10643275704402246868)
XLA Ops:
  10.4 43.2 %all-reduce.11 = (bf16[2048]{0:T(1024)(128)(2,1)S(1)}, bf16[2048]{0:T(1024)(128)(2,1)S(1)}) all-reduce(bf16[2048]{0:T(1024)(128)(2,1)S(1)} %dynamic-update-slice, bf16[2048]{0:T(1024)(128)(2,1)S(1)} %dynamic-update-slice.1), channel_id=1, replica_groups=mesh['rows'=4,'mp'=8] {'rows','mp'}, use_global_device_ids=true, to_apply=%add.6 | all-reduce | flops 4096 | bytes 16384
  59.7 29.9 %all-gather.10.cloned.1.call-done = bf16[2048,1920]{1,0:T(8,128)(2,1)} async-done(((bf16[64,1920]{1,0:T(8,128)(2,1)}), bf16[2048,1920]{1,0:T(8,128)(2,1)}) %all-gather.10.cloned.1.call-update) | async-done | bytes 7864336 | tf_op jit(solution)/shard_map/all_gather | solution.py:156
  97.7 58.8 %all-gather.14.cloned.1.call-done = bf16[1280,2048]{1,0:T(8,128)(2,1)} async-done(((bf16[40,2048]{1,0:T(8,128)(2,1)}), bf16[1280,2048]{1,0:T(8,128)(2,1)}) %all-gather.14.cloned.1.call-update) | async-done | bytes 5242896 | tf_op jit(solution)/shard_map/all_gather | solution.py:157
  156.5 82.6 %all-gather.8.cloned.1.call-done = bf16[2048,2048]{1,0:T(8,128)(2,1)} async-done(((bf16[256,2048]{1,0:T(8,128)(2,1)}), bf16[2048,2048]{1,0:T(8,128)(2,1)}) %all-gather.8.cloned.1.call-update) | async-done | bytes 8388624 | tf_op jit(solution)/shard_map/all_gather | solution.py:169
  239.1 34.5 %all-gather.12.cloned.1.call-done = bf16[2048,640]{1,0:T(8,128)(2,1)} async-done(((bf16[256,640]{1,0:T(8,128)(2,1)}), bf16[2048,640]{1,0:T(8,128)(2,1)}) %all-gather.12.cloned.1.call-update) | async-done | bytes 2621456 | tf_op jit(solution)/shard_map/all_gather | solution.py:170
  281.5 150.9 %while.42 = (s32[]{:T(128)}, f32[2048,2048]{1,0:T(8,128)}, bf16[10,512,64]{1,2,0:T(8,128)(2,1)}, bf16[10,512,64]{1,2,0:T(8,128)(2,1)}, f32[10,512]{1,0:T(8,128)S...) while((s32[]{:T(128)}, f32[2048,2048]{1,0:T(8,128)}, ...), condition=%wide.region_14.15_spmd, body=%wide.region_1.14_spmd.sunk | while | flops 547767360 | bytes 25982072 | solution.py:202
  432.5 169.8 %reduce-scatter.8.cloned.1.call-done = f32[256,2048]{1,0:T(8,128)} async-done(((f32[2048,2048]{1,0:T(8,128)}), f32[256,2048]{1,0:T(8,128)}) %reduce-scatter.8.cloned.1.call-update) | async-done | bytes 2097168 | tf_op jit(solution)/shard_map/reduce_scatter | solution.py:205
  622.9 64.7 %all-gather.16.cloned.1.call-done = bf16[2048,2048]{1,0:T(8,128)(2,1)} async-done(((bf16[256,2048]{1,0:T(8,128)(2,1)}), bf16[2048,2048]{1,0:T(8,128)(2,1)}) %all-gather.16.cloned.1.call-update) | async-done | bytes 8388624 | tf_op jit(solution)/shard_map/all_gather | solution.py:209
  687.6 11.8 fusion.167
  707.9 62.5 %all-gather.18.cloned.1.call-done = bf16[2048,2048]{1,0:T(8,128)(2,1)} async-done(((bf16[256,2048]{1,0:T(8,128)(2,1)}), bf16[2048,2048]{1,0:T(8,128)(2,1)}) %all-gather.18.cloned.1.call-update) | async-done | bytes 8388624 | tf_op jit(solution)/shard_map/all_gather | solution.py:225
  770.4 15.7 multiply_convert_fusion.2
  786.1 13.3 fusion.168
  799.4 14.1 convolution_add_fusion.2
  824.5 156.0 %reduce-scatter.12.cloned.1.call-done = f32[256,2048]{1,0:T(8,128)} async-done(((f32[2048,2048]{1,0:T(8,128)}), f32[256,2048]{1,0:T(8,128)}) %reduce-scatter.12.cloned.1.call-update) | async-done | bytes 2097168 | tf_op jit(solution)/shard_map/reduce_scatter | solution.py:241
  983.3 87.6 %reduce-scatter.10.cloned.1.call-done = bf16[256,2048]{1,0:T(8,128)(2,1)} async-done(((bf16[2048,2048]{1,0:T(8,128)(2,1)}), bf16[256,2048]{1,0:T(8,128)(2,1)}) %reduce-scatter.10.cloned.1.call-update) | async-done | bytes 1048592 | tf_op jit(solution)/shard_map/reduce_scatter | solution.py:214
  1077.9 78.2 %all-gather.20.cloned.1.call-done = bf16[2048,2048]{1,0:T(8,128)(2,1)} async-done(((bf16[256,2048]{1,0:T(8,128)(2,1)}), bf16[2048,2048]{1,0:T(8,128)(2,1)}) %all-gather.20.cloned.1.call-update) | async-done | bytes 8388624 | tf_op jit(solution)/shard_map/all_gather | solution.py:249
  1177.5 293.2 %while.43 = (s32[]{:T(128)}, f32[2048,2048]{1,0:T(8,128)}, f32[2048,640]{0,1:T(8,128)}, f32[2048,1280]{0,1:T(8,128)}, f32[1280,2048]{1,0:T(8,128)}, /*index=5*/s...) while((s32[]{:T(128)}, f32[2048,2048]{1,0:T(8,128)}, ...), condition=%wide.region_32.33_spmd, body=%wide.region_23.32_spmd.sunk | while | flops 1220625536 | bytes 55792484 | solution.py:298
  1470.7 12.2 convolution_convert_fusion.1
  1512.9 21.2 reduce-scatter.16.cloned.1.call-done
  1546.4 180.2 %all-reduce.15.cloned.1.call-done = (bf16[2048,768]{1,0:T(8,128)(2,1)}, bf16[2048,768]{1,0:T(8,128)(2,1)}, bf16[768,2048]{1,0:T(8,128)(2,1)}) async-done(((bf16[2048,768]{1,0:T(8,128)(2,1)}, bf16[2048,768]{1,0:T(8,128)(2,1)}, bf16[768,2048]{1,0:T(8,128)(2,1)}), (bf16[2048,768]{1,0:T(8,128)(2,1)}, bf16[2048,768]{1,0:T(8,128)(2,1)}, bf16[768,2048]{1,0:T(8,128)(2,1)})) %all-reduce.15.cloned.1.call-update) | async-done | bytes 9437200 | tf_op jit(solution)/shard_map/psum | solution.py:333
  1739.3 158.0 %reduce-scatter.14.cloned.1.call-done = f32[256,2048]{1,0:T(8,128)} async-done(((f32[2048,2048]{1,0:T(8,128)}), f32[256,2048]{1,0:T(8,128)}) %reduce-scatter.14.cloned.1.call-update) | async-done | bytes 2097168 | tf_op jit(solution)/shard_map/reduce_scatter | solution.py:302
  1902.3 38.8 %all-reduce.10 = (f32[2048]{0:T(1024)S(1)}, f32[2048]{0:T(1024)S(1)}) all-reduce(f32[2048]{0:T(1024)S(1)} %get-tuple-element.1396, f32[2048]{0:T(1024)S(1)} %copy-done.14), channel_id=9, replica_groups=mesh['rows'=4,'mp'=8] {'rows','mp'}, use_global_device_ids=true, to_apply=%region_42.43.clone | all-reduce | flops 4096 | bytes 32768
  1947.0 109.4 %reduce-scatter.20.cloned.1.call-done = f32[40,2048]{1,0:T(8,128)} async-done(((f32[1280,2048]{1,0:T(8,128)}), f32[40,2048]{1,0:T(8,128)}) %reduce-scatter.20.cloned.1.call-update) | async-done | bytes 327696 | tf_op jit(solution)/shard_map/reduce_scatter | solution.py:328
  2056.3 174.8 %reduce-scatter.18.cloned.1.call-done = f32[64,1920]{1,0:T(8,128)} async-done(((f32[2048,1920]{1,0:T(8,128)}), f32[64,1920]{1,0:T(8,128)}) %reduce-scatter.18.cloned.1.call-update) | async-done | bytes 491536 | tf_op jit(solution)/shard_map/reduce_scatter | solution.py:327
  (506 shorter events, 702.0 us)
Async XLA Ops:
  7.2 763.2 %copy-start = (bf16[768,2048]{1,0:T(8,128)(2,1)S(1)}, bf16[768,2048]{1,0:T(8,128)(2,1)}, u32[]{:S(2)}) copy-start(bf16[768,2048]{1,0:T(8,128)(2,1)} %param.33) | copy-start | bytes 9437188
  7.2 82.5 %all-gather.10.cloned.1.call-start = ((), (), s32[]{:S(2)}) async-start(), calls=%async_computation.8 | async-start | bytes 8110080 | tf_op jit(solution)/shard_map/all_gather | solution.py:156
  7.9 148.6 %all-gather.14.cloned.1.call-start = ((), (), s32[]{:S(2)}) async-start(), calls=%async_computation.10 | async-start | bytes 5406720 | tf_op jit(solution)/shard_map/all_gather | solution.py:157
  8.7 230.4 %all-gather.8.cloned.1.call-start = ((), (), s32[]{:S(2)}) async-start(), calls=%async_computation.7 | async-start | bytes 9437184 | tf_op jit(solution)/shard_map/all_gather | solution.py:169
  58.8 214.7 %all-gather.12.cloned.1.call-start = ((), (), s32[]{:S(2)}) async-start(), calls=%async_computation.9 | async-start | bytes 2949120 | tf_op jit(solution)/shard_map/all_gather | solution.py:170
  97.4 504.8 %reduce-scatter.8.cloned.1.call-start = ((), (), s32[]{:S(2)}) async-start(), calls=%async_computation.11 | async-start | bytes 18874368 | tf_op jit(solution)/shard_map/reduce_scatter | solution.py:205
  432.4 255.2 %all-gather.16.cloned.1.call-start = ((), (), s32[]{:S(2)}) async-start(), calls=%async_computation.12 | async-start | bytes 9437184 | tf_op jit(solution)/shard_map/all_gather | solution.py:209
  607.0 163.4 %all-gather.18.cloned.1.call-start = ((), (), s32[]{:S(2)}) async-start(), calls=%async_computation.14 | async-start | bytes 9437184 | tf_op jit(solution)/shard_map/all_gather | solution.py:225
  622.7 357.9 %reduce-scatter.12.cloned.1.call-start = ((), (), s32[]{:S(2)}) async-start(), calls=%async_computation.15 | async-start | bytes 18874368 | tf_op jit(solution)/shard_map/reduce_scatter | solution.py:241
  813.6 257.2 %reduce-scatter.10.cloned.1.call-start = ((), (), s32[]{:S(2)}) async-start(), calls=%async_computation.13 | async-start | bytes 9437184 | tf_op jit(solution)/shard_map/reduce_scatter | solution.py:214
  824.4 156.1 %copy-start.4 = (f32[256,2048]{1,0:T(8,128)S(1)}, f32[256,2048]{1,0:T(8,128)}, u32[]{:S(2)}) copy-start(f32[256,2048]{1,0:T(8,128)} %copy-done.3) | copy-start | bytes 6291460
  824.5 246.3 %copy-start.7 = (bf16[256,2048]{1,0:T(8,128)(2,1)S(1)}, bf16[256,2048]{1,0:T(8,128)(2,1)}, u32[]{:S(2)}) copy-start(bf16[256,2048]{1,0:T(8,128)(2,1)} %param.24) | copy-start | bytes 3145732
  824.5 331.6 %all-gather.20.cloned.1.call-start = ((), (), s32[]{:S(2)}) async-start(), calls=%async_computation.16 | async-start | bytes 9437184 | tf_op jit(solution)/shard_map/all_gather | solution.py:249
  1075.5 458.6 %reduce-scatter.16.cloned.1.call-start = ((), (), s32[]{:S(2)}) async-start(), calls=%async_computation.18 | async-start | bytes 5898240 | tf_op jit(solution)/shard_map/reduce_scatter | solution.py:303
  1470.7 255.9 %all-reduce.15.cloned.1.call-start = ((), (), s32[]{:S(2)}) async-start(), calls=%async_computation.21 | async-start | bytes 18874368 | tf_op jit(solution)/shard_map/psum | solution.py:333
  1499.9 397.3 %reduce-scatter.14.cloned.1.call-start = ((), (), s32[]{:S(2)}) async-start(), calls=%async_computation.17 | async-start | bytes 18874368 | tf_op jit(solution)/shard_map/reduce_scatter | solution.py:302
  1500.7 555.7 %reduce-scatter.20.cloned.1.call-start = ((), (), s32[]{:S(2)}) async-start(), calls=%async_computation.20 | async-start | bytes 10813440 | tf_op jit(solution)/shard_map/reduce_scatter | solution.py:328
  1501.2 729.9 %reduce-scatter.18.cloned.1.call-start = ((), (), s32[]{:S(2)}) async-start(), calls=%async_computation.19 | async-start | bytes 16220160 | tf_op jit(solution)/shard_map/reduce_scatter | solution.py:327
  1735.7 161.5 %copy-start.5 = (bf16[256,2048]{1,0:T(8,128)(2,1)S(1)}, bf16[256,2048]{1,0:T(8,128)(2,1)}, u32[]{:S(2)}) copy-start(bf16[256,2048]{1,0:T(8,128)(2,1)} %param.23) | copy-start | bytes 3145732
  1735.7 161.5 %copy-start.13 = (f32[2048]{0:T(1024)S(1)}, f32[2048]{0:T(1024)}, u32[]{:S(2)}) copy-start(f32[2048]{0:T(1024)} %copy-done.12) | copy-start | bytes 24580
  1735.7 161.5 %copy-start.16 = (f32[256]{0:T(256)S(1)}, f32[256]{0:T(256)}, u32[]{:S(2)}) copy-start(f32[256]{0:T(256)} %copy-done.15) | copy-start | bytes 3076
  1739.2 163.1 %copy-start.14 = (f32[2048]{0:T(1024)S(1)}, f32[2048]{0:T(1024)}, u32[]{:S(2)}) copy-start(f32[2048]{0:T(1024)} %get-tuple-element.1394) | copy-start | bytes 24580
  1739.3 203.1 %copy-start.17 = (f32[256]{0:T(256)S(1)}, f32[256]{0:T(256)}, u32[]{:S(2)}) copy-start(f32[256]{0:T(256)} %get-tuple-element.1493) | copy-start | bytes 3076
  1942.3 288.8 %copy-start.1 = (bf16[768,2048]{1,0:T(8,128)(2,1)S(1)}, bf16[768,2048]{1,0:T(8,128)(2,1)}, u32[]{:S(2)}) copy-start(bf16[768,2048]{1,0:T(8,128)(2,1)} %param.33) | copy-start | bytes 9437188
  (18 other events, 233.7 us)
Sparse Core Ops, SparseCore 0:
  11.0 78.5 all-gather.9
  92.5 63.9 all-gather.13
  158.1 80.9 all-gather.7
  241.1 32.3 all-gather.11
  432.5 169.6 reduce-scatter.7
  607.1 80.4 all-gather.15
  689.8 80.5 all-gather.17
  813.7 166.7 reduce-scatter.11
  982.8 87.9 reduce-scatter.9
  1075.6 80.4 all-gather.19
  1470.8 63.3 reduce-scatter.15
  1538.4 188.0 all-reduce.14
  1728.9 168.2 reduce-scatter.13
  1899.9 156.3 reduce-scatter.19
  2062.8 168.3 reduce-scatter.17
where the time goes:
time: 2250 us; the launch traced here: 2240 us
  waiting for transfers between devices  1470 us (65%)
  matrix products  430 us (19%)
  other arithmetic  110 us (5%)
  blocking collectives  91.9 us (4%)
  local copies, waits for them, and re-layouts  82.2 us (4%)
  loops' own time  36 us (2%)
    psum x1, waiting for transfers between devices, on_device(): lax.psum(gate_grad.astype(jnp.bfloat16), 'rows').astype(jnp.float32)  180 us
    reduce_scatter x1, waiting for transfers between devices, on_device(): lax.psum_scatter(qkv_grad_full, ('rows', 'mp'), scatter_dimension=0, tile...  175 us
    reduce_scatter x1, waiting for transfers between devices, on_device(): lax.psum_scatter(attn_partial, 'mp', scatter_dimension=0, tiled=True)  170 us
    reduce_scatter x1, waiting for transfers between devices, on_device(): lax.psum_scatter(input_partial, 'mp', scatter_dimension=0, tiled=True)  158 us
    reduce_scatter x1, waiting for transfers between devices, on_device(): lax.psum_scatter(mid_partial, 'mp', scatter_dimension=0, tiled=True)  156 us
    reduce_scatter x1, waiting for transfers between devices, on_device(): lax.psum_scatter(o_grad_w, ('rows', 'mp'), scatter_dimension=0, tiled=True)  109 us
    reduce_scatter x1, waiting for transfers between devices, on_device(): lax.psum_scatter(ffn_part.astype(jnp.bfloat16), 'mp', scatter_dimension=0...  87.6 us
    all_gather x1, waiting for transfers between devices, on_device(): lax.all_gather(normed_one, 'mp', axis=0, tiled=True)  82.6 us
  transfers between devices with their start and end apart: 15, of which 15 were waited for; matrix products, arithmetic and copies ran while one was open for 6% of the time, Pallas kernels for 0%

commit v1 on v0

--- a/solution.py
+++ b/solution.py
@@ -330,7 +330,7 @@
         lax.psum_scatter(ffn_gain_part, ("rows", "mp"), scatter_dimension=0, tiled=True),
     )
     gate_grad, up_grad, down_grad = (
-        lax.psum(gate_grad.astype(jnp.bfloat16), "rows").astype(jnp.float32),
+        jnp.sum(lax.all_gather(gate_grad.astype(jnp.bfloat16), "rows"), axis=0).astype(jnp.float32),
         lax.psum(up_grad.astype(jnp.bfloat16), "rows").astype(jnp.float32),
         lax.psum(down_grad.astype(jnp.bfloat16), "rows").astype(jnp.float32),
     )

time: 2250 us -> 2320 us (1.031)
  waiting for transfers between devices: 1470 us -> 1530 us
    all_gather x0 -> x1, waiting for transfers between devices: none -> 116 us  [on_device(): lax.all_gather(gate_grad.astype(jnp.bfloat16), 'rows')]
    psum x1, waiting for transfers between devices: 180 us -> 129 us  [on_device(): lax.psum(up_grad.astype(jnp.bfloat16), 'rows').astype(jnp.float32)]
  transfers between devices with their start and end apart: 15 -> 16, of which waited for: 15 -> 16; matrix products, arithmetic and copies ran while one was open for 6% -> 6% of each run, Pallas kernels for 0% -> 0%
where the time goes in v1:
time: 2320 us; the launch traced here: 2310 us
  waiting for transfers between devices  1530 us (66%)
  matrix products  431 us (19%)
  other arithmetic  120 us (5%)
  blocking collectives  92.3 us (4%)
  local copies, waits for them, and re-layouts  84.3 us (4%)
  loops' own time  36 us (2%)
    reduce_scatter x1, waiting for transfers between devices, on_device(): lax.psum_scatter(qkv_grad_full, ('rows', 'mp'), scatter_dimension=0, tile...  175 us
    reduce_scatter x1, waiting for transfers between devices, on_device(): lax.psum_scatter(attn_partial, 'mp', scatter_dimension=0, tiled=True)  170 us
    reduce_scatter x1, waiting for transfers between devices, on_device(): lax.psum_scatter(input_partial, 'mp', scatter_dimension=0, tiled=True)  156 us
    reduce_scatter x1, waiting for transfers between devices, on_device(): lax.psum_scatter(mid_partial, 'mp', scatter_dimension=0, tiled=True)  156 us
    psum x1, waiting for transfers between devices, on_device(): lax.psum(up_grad.astype(jnp.bfloat16), 'rows').astype(jnp.float32)  129 us
    all_gather x1, waiting for transfers between devices, on_device(): lax.all_gather(gate_grad.astype(jnp.bfloat16), 'rows')  116 us
    reduce_scatter x1, waiting for transfers between devices, on_device(): lax.psum_scatter(o_grad_w, ('rows', 'mp'), scatter_dimension=0, tiled=True)  109 us
    reduce_scatter x1, waiting for transfers between devices, on_device(): lax.psum_scatter(ffn_part.astype(jnp.bfloat16), 'mp', scatter_dimension=0...  87.5 us
  transfers between devices with their start and end apart: 16, of which 16 were waited for; matrix products, arithmetic and copies ran while one was open for 6% of the time, Pallas kernels for 0%

profile of v1, /device:TPU:0, one launch (start us, length us, event | category | flops | bytes accessed | tf_op | source)
XLA Modules:
  0.0 2311.9 jit_solution(7410365720003434355)
XLA Ops:
  10.4 43.2 %all-reduce.11 = (bf16[2048]{0:T(1024)(128)(2,1)S(1)}, bf16[2048]{0:T(1024)(128)(2,1)S(1)}) all-reduce(bf16[2048]{0:T(1024)(128)(2,1)S(1)} %dynamic-update-slice, bf16[2048]{0:T(1024)(128)(2,1)S(1)} %dynamic-update-slice.1), channel_id=1, replica_groups=mesh['rows'=4,'mp'=8] {'rows','mp'}, use_global_device_ids=true, to_apply=%add.6 | all-reduce | flops 4096 | bytes 16384
  59.8 29.9 %all-gather.12.cloned.1.call-done = bf16[2048,1920]{1,0:T(8,128)(2,1)} async-done(((bf16[64,1920]{1,0:T(8,128)(2,1)}), bf16[2048,1920]{1,0:T(8,128)(2,1)}) %all-gather.12.cloned.1.call-update) | async-done | bytes 7864336 | tf_op jit(solution)/shard_map/all_gather | solution.py:156
  97.7 58.8 %all-gather.16.cloned.1.call-done = bf16[1280,2048]{1,0:T(8,128)(2,1)} async-done(((bf16[40,2048]{1,0:T(8,128)(2,1)}), bf16[1280,2048]{1,0:T(8,128)(2,1)}) %all-gather.16.cloned.1.call-update) | async-done | bytes 5242896 | tf_op jit(solution)/shard_map/all_gather | solution.py:157
  156.5 82.6 %all-gather.10.cloned.1.call-done = bf16[2048,2048]{1,0:T(8,128)(2,1)} async-done(((bf16[256,2048]{1,0:T(8,128)(2,1)}), bf16[2048,2048]{1,0:T(8,128)(2,1)}) %all-gather.10.cloned.1.call-update) | async-done | bytes 8388624 | tf_op jit(solution)/shard_map/all_gather | solution.py:169
  239.1 34.5 %all-gather.14.cloned.1.call-done = bf16[2048,640]{1,0:T(8,128)(2,1)} async-done(((bf16[256,640]{1,0:T(8,128)(2,1)}), bf16[2048,640]{1,0:T(8,128)(2,1)}) %all-gather.14.cloned.1.call-update) | async-done | bytes 2621456 | tf_op jit(solution)/shard_map/all_gather | solution.py:170
  281.4 150.8 %while.42 = (s32[]{:T(128)}, f32[2048,2048]{1,0:T(8,128)}, bf16[10,512,64]{1,2,0:T(8,128)(2,1)}, bf16[10,512,64]{1,2,0:T(8,128)(2,1)}, f32[10,512]{1,0:T(8,128)S...) while((s32[]{:T(128)}, f32[2048,2048]{1,0:T(8,128)}, ...), condition=%wide.region_14.15_spmd, body=%wide.region_1.14_spmd.sunk | while | flops 547767360 | bytes 25982072 | solution.py:202
  432.3 169.8 %reduce-scatter.8.cloned.1.call-done = f32[256,2048]{1,0:T(8,128)} async-done(((f32[2048,2048]{1,0:T(8,128)}), f32[256,2048]{1,0:T(8,128)}) %reduce-scatter.8.cloned.1.call-update) | async-done | bytes 2097168 | tf_op jit(solution)/shard_map/reduce_scatter | solution.py:205
  622.8 64.6 %all-gather.18.cloned.1.call-done = bf16[2048,2048]{1,0:T(8,128)(2,1)} async-done(((bf16[256,2048]{1,0:T(8,128)(2,1)}), bf16[2048,2048]{1,0:T(8,128)(2,1)}) %all-gather.18.cloned.1.call-update) | async-done | bytes 8388624 | tf_op jit(solution)/shard_map/all_gather | solution.py:209
  707.8 62.5 %all-gather.20.cloned.1.call-done = bf16[2048,2048]{1,0:T(8,128)(2,1)} async-done(((bf16[256,2048]{1,0:T(8,128)(2,1)}), bf16[2048,2048]{1,0:T(8,128)(2,1)}) %all-gather.20.cloned.1.call-update) | async-done | bytes 8388624 | tf_op jit(solution)/shard_map/all_gather | solution.py:225
  770.3 15.7 multiply_convert_fusion.2
  786.0 13.2 fusion.168
  799.2 14.1 convolution_add_fusion.2
  824.3 155.9 %reduce-scatter.12.cloned.1.call-done = f32[256,2048]{1,0:T(8,128)} async-done(((f32[2048,2048]{1,0:T(8,128)}), f32[256,2048]{1,0:T(8,128)}) %reduce-scatter.12.cloned.1.call-update) | async-done | bytes 2097168 | tf_op jit(solution)/shard_map/reduce_scatter | solution.py:241
  982.9 87.5 %reduce-scatter.10.cloned.1.call-done = bf16[256,2048]{1,0:T(8,128)(2,1)} async-done(((bf16[2048,2048]{1,0:T(8,128)(2,1)}), bf16[256,2048]{1,0:T(8,128)(2,1)}) %reduce-scatter.10.cloned.1.call-update) | async-done | bytes 1048592 | tf_op jit(solution)/shard_map/reduce_scatter | solution.py:214
  1077.6 78.1 %all-gather.22.cloned.1.call-done = bf16[2048,2048]{1,0:T(8,128)(2,1)} async-done(((bf16[256,2048]{1,0:T(8,128)(2,1)}), bf16[2048,2048]{1,0:T(8,128)(2,1)}) %all-gather.22.cloned.1.call-update) | async-done | bytes 8388624 | tf_op jit(solution)/shard_map/all_gather | solution.py:249
  1177.2 293.0 %while.43 = (s32[]{:T(128)}, f32[2048,2048]{1,0:T(8,128)}, f32[2048,640]{0,1:T(8,128)}, f32[2048,1280]{0,1:T(8,128)}, f32[1280,2048]{1,0:T(8,128)}, /*index=5*/s...) while((s32[]{:T(128)}, f32[2048,2048]{1,0:T(8,128)}, ...), condition=%wide.region_32.33_spmd, body=%wide.region_23.32_spmd.sunk | while | flops 1220625536 | bytes 55792484 | solution.py:298
  1470.3 12.1 convolution_convert_fusion.1
  1516.2 18.3 reduce-scatter.16.cloned.1.call-done
  1546.7 128.8 %all-reduce.15.cloned.1.call-done = (bf16[2048,768]{1,0:T(8,128)(2,1)}, bf16[768,2048]{1,0:T(8,128)(2,1)}) async-done(((bf16[2048,768]{1,0:T(8,128)(2,1)}, bf16[768,2048]{1,0:T(8,128)(2,1)}), (bf16[2048,768]{1,0:T(8,128)(2,1)}, bf16[768,2048]{1,0:T(8,128)(2,1)})) %all-reduce.15.cloned.1.call-update) | async-done | bytes 6291472 | tf_op jit(solution)/shard_map/psum | solution.py:334
  1684.4 116.2 %all-gather.24.cloned.1.call-done = bf16[8192,768]{1,0:T(8,128)(2,1)} async-done(((bf16[2048,768]{1,0:T(8,128)(2,1)}), bf16[8192,768]{1,0:T(8,128)(2,1)}) %all-gather.24.cloned.1.call-update) | async-done | bytes 12582928 | tf_op jit(solution)/shard_map/all_gather | solution.py:333
  1814.8 156.2 %reduce-scatter.14.cloned.1.call-done = f32[256,2048]{1,0:T(8,128)} async-done(((f32[2048,2048]{1,0:T(8,128)}), f32[256,2048]{1,0:T(8,128)}) %reduce-scatter.14.cloned.1.call-update) | async-done | bytes 2097168 | tf_op jit(solution)/shard_map/reduce_scatter | solution.py:302
  1976.2 39.2 %all-reduce.10 = (f32[2048]{0:T(1024)S(1)}, f32[2048]{0:T(1024)S(1)}) all-reduce(f32[2048]{0:T(1024)S(1)} %get-tuple-element.1396, f32[2048]{0:T(1024)S(1)} %copy-done.13), channel_id=10, replica_groups=mesh['rows'=4,'mp'=8] {'rows','mp'}, use_global_device_ids=true, to_apply=%region_42.43.clone | all-reduce | flops 4096 | bytes 32768
  2021.2 109.0 %reduce-scatter.20.cloned.1.call-done = f32[40,2048]{1,0:T(8,128)} async-done(((f32[1280,2048]{1,0:T(8,128)}), f32[40,2048]{1,0:T(8,128)}) %reduce-scatter.20.cloned.1.call-update) | async-done | bytes 327696 | tf_op jit(solution)/shard_map/reduce_scatter | solution.py:328
  2130.2 174.7 %reduce-scatter.18.cloned.1.call-done = f32[64,1920]{1,0:T(8,128)} async-done(((f32[2048,1920]{1,0:T(8,128)}), f32[64,1920]{1,0:T(8,128)}) %reduce-scatter.18.cloned.1.call-update) | async-done | bytes 491536 | tf_op jit(solution)/shard_map/reduce_scatter | solution.py:327
  (508 shorter events, 728.1 us)
Async XLA Ops:
  7.2 763.1 %copy-start = (bf16[768,2048]{1,0:T(8,128)(2,1)S(1)}, bf16[768,2048]{1,0:T(8,128)(2,1)}, u32[]{:S(2)}) copy-start(bf16[768,2048]{1,0:T(8,128)(2,1)} %param.33) | copy-start | bytes 9437188
  7.2 82.4 %all-gather.12.cloned.1.call-start = ((), (), s32[]{:S(2)}) async-start(), calls=%async_computation.8 | async-start | bytes 8110080 | tf_op jit(solution)/shard_map/all_gather | solution.py:156
  7.9 148.6 %all-gather.16.cloned.1.call-start = ((), (), s32[]{:S(2)}) async-start(), calls=%async_computation.10 | async-start | bytes 5406720 | tf_op jit(solution)/shard_map/all_gather | solution.py:157
  8.7 230.4 %all-gather.10.cloned.1.call-start = ((), (), s32[]{:S(2)}) async-start(), calls=%async_computation.7 | async-start | bytes 9437184 | tf_op jit(solution)/shard_map/all_gather | solution.py:169
  58.9 214.7 %all-gather.14.cloned.1.call-start = ((), (), s32[]{:S(2)}) async-start(), calls=%async_computation.9 | async-start | bytes 2949120 | tf_op jit(solution)/shard_map/all_gather | solution.py:170
  97.4 504.7 %reduce-scatter.8.cloned.1.call-start = ((), (), s32[]{:S(2)}) async-start(), calls=%async_computation.11 | async-start | bytes 18874368 | tf_op jit(solution)/shard_map/reduce_scatter | solution.py:205
  432.2 255.2 %all-gather.18.cloned.1.call-start = ((), (), s32[]{:S(2)}) async-start(), calls=%async_computation.12 | async-start | bytes 9437184 | tf_op jit(solution)/shard_map/all_gather | solution.py:209
  606.9 163.4 %all-gather.20.cloned.1.call-start = ((), (), s32[]{:S(2)}) async-start(), calls=%async_computation.14 | async-start | bytes 9437184 | tf_op jit(solution)/shard_map/all_gather | solution.py:225
  622.5 357.7 %reduce-scatter.12.cloned.1.call-start = ((), (), s32[]{:S(2)}) async-start(), calls=%async_computation.15 | async-start | bytes 18874368 | tf_op jit(solution)/shard_map/reduce_scatter | solution.py:241
  813.3 257.2 %reduce-scatter.10.cloned.1.call-start = ((), (), s32[]{:S(2)}) async-start(), calls=%async_computation.13 | async-start | bytes 9437184 | tf_op jit(solution)/shard_map/reduce_scatter | solution.py:214
  824.3 246.2 %copy-start.7 = (bf16[256,2048]{1,0:T(8,128)(2,1)S(1)}, bf16[256,2048]{1,0:T(8,128)(2,1)}, u32[]{:S(2)}) copy-start(bf16[256,2048]{1,0:T(8,128)(2,1)} %param.24) | copy-start | bytes 3145732
  824.3 331.5 %all-gather.22.cloned.1.call-start = ((), (), s32[]{:S(2)}) async-start(), calls=%async_computation.16 | async-start | bytes 9437184 | tf_op jit(solution)/shard_map/all_gather | solution.py:249
  1075.2 459.3 %reduce-scatter.16.cloned.1.call-start = ((), (), s32[]{:S(2)}) async-start(), calls=%async_computation.18 | async-start | bytes 5898240 | tf_op jit(solution)/shard_map/reduce_scatter | solution.py:303
  1470.3 205.3 %all-reduce.15.cloned.1.call-start = ((), (), s32[]{:S(2)}) async-start(), calls=%async_computation.22 | async-start | bytes 12582912 | tf_op jit(solution)/shard_map/psum | solution.py:334
  1490.9 309.6 %all-gather.24.cloned.1.call-start = ((), (), s32[]{:S(2)}) async-start(), calls=%async_computation.21 | async-start | bytes 15728640 | tf_op jit(solution)/shard_map/all_gather | solution.py:333
  1503.3 467.7 %reduce-scatter.14.cloned.1.call-start = ((), (), s32[]{:S(2)}) async-start(), calls=%async_computation.17 | async-start | bytes 18874368 | tf_op jit(solution)/shard_map/reduce_scatter | solution.py:302
  1503.9 626.3 %reduce-scatter.20.cloned.1.call-start = ((), (), s32[]{:S(2)}) async-start(), calls=%async_computation.20 | async-start | bytes 10813440 | tf_op jit(solution)/shard_map/reduce_scatter | solution.py:328
  1504.5 800.5 %reduce-scatter.18.cloned.1.call-start = ((), (), s32[]{:S(2)}) async-start(), calls=%async_computation.19 | async-start | bytes 16220160 | tf_op jit(solution)/shard_map/reduce_scatter | solution.py:327
  1809.6 161.4 %copy-start.5 = (bf16[256,2048]{1,0:T(8,128)(2,1)S(1)}, bf16[256,2048]{1,0:T(8,128)(2,1)}, u32[]{:S(2)}) copy-start(bf16[256,2048]{1,0:T(8,128)(2,1)} %param.23) | copy-start | bytes 3145732
  1809.6 161.4 %copy-start.12 = (f32[2048]{0:T(1024)S(1)}, f32[2048]{0:T(1024)}, u32[]{:S(2)}) copy-start(f32[2048]{0:T(1024)} %copy-done.11) | copy-start | bytes 24580
  1809.6 161.4 %copy-start.15 = (f32[256]{0:T(256)S(1)}, f32[256]{0:T(256)}, u32[]{:S(2)}) copy-start(f32[256]{0:T(256)} %copy-done.14) | copy-start | bytes 3076
  1814.8 161.4 %copy-start.13 = (f32[2048]{0:T(1024)S(1)}, f32[2048]{0:T(1024)}, u32[]{:S(2)}) copy-start(f32[2048]{0:T(1024)} %get-tuple-element.1394) | copy-start | bytes 24580
  1814.8 201.8 %copy-start.16 = (f32[256]{0:T(256)S(1)}, f32[256]{0:T(256)}, u32[]{:S(2)}) copy-start(f32[256]{0:T(256)} %get-tuple-element.1492) | copy-start | bytes 3076
  2016.5 288.4 %copy-start.1 = (bf16[768,2048]{1,0:T(8,128)(2,1)S(1)}, bf16[768,2048]{1,0:T(8,128)(2,1)}, u32[]{:S(2)}) copy-start(bf16[768,2048]{1,0:T(8,128)(2,1)} %param.33) | copy-start | bytes 9437188
  (18 other events, 370.1 us)
Sparse Core Ops, SparseCore 0:
  11.0 78.5 all-gather.11
  92.5 63.9 all-gather.15
  158.1 80.9 all-gather.9
  241.1 32.3 all-gather.13
  432.4 169.7 reduce-scatter.7
  607.0 80.4 all-gather.17
  689.6 80.5 all-gather.19
  813.4 166.7 reduce-scatter.11
  982.5 87.9 reduce-scatter.9
  1075.3 80.3 all-gather.21
  1470.4 64.0 reduce-scatter.15
  1538.4 137.1 all-reduce.14
  1678.0 122.5 all-gather.23
  1802.7 168.2 reduce-scatter.13
  1973.7 156.3 reduce-scatter.19
  2136.6 168.2 reduce-scatter.17
